TPU v7x, 32 devices: a whole 2x2x4 slice. The times are simulated.
32 devices in a mesh: layer: 4 (over y, x), row: 2 (over core), col: 4 (over z).
Axes of the slice: x: 2, y: 2, z: 4, core: 2. Of those that a mesh axis runs over, the one named last changes fastest.
Arguments:
- blocks: bfloat16 [13, 512, 128, 128], P(None, ('row', 'col'), 'layer'), may hold values from -0.29882812 to 0.29882812
- presence: int32 [13, 512], P(None, ('row', 'col')), may hold values from 0 to 1, as said below
Outputs:
- purified: bfloat16 [13, 512, 128, 128], P(None, ('row', 'col'), 'layer')
Inputs may be any that keep to these rules, and one draw needn't show every extreme that they name: `presence`: the tile on offset 0 is present in every block row.
All inputs are finite; a program needn't handle non-finite values.
Results may differ from a plain program's by a relative error of at most 0.01.
Values may be sent and summed in bfloat16 or wider, within the bound.
A program may use at most 320 MiB of HBM per device.

v0:
```python
import functools

import jax
import jax.numpy as jnp
from jax import lax
from jax.experimental import pallas as pl
from jax.experimental.pallas import tpu as pltpu
from jax.sharding import PartitionSpec as P

BAND = 3
FAR = 160
CHUNKS = 8
WIDTH = 2 * BAND + 1
MESH = pl.DeviceIdType.MESH


def offset_table(total_rows):
    values = list(range(-BAND, BAND + 1))
    values = values + [FAR - 1, FAR, FAR + 1, -FAR - 1, -FAR, -FAR + 1]
    return [value % total_rows for value in values]


def pair_table(offsets, total_rows):
    by_target = []
    for target in offsets:
        entries = []
        for left_index, left in enumerate(offsets):
            for right_index, right in enumerate(offsets):
                if (left + right) % total_rows == target:
                    entries.append((left_index, right_index))
        by_target.append(entries)
    return by_target


def runs_of(indices):
    runs = []
    for position, index in enumerate(indices):
        if runs and runs[-1][1] + runs[-1][2] == index:
            runs[-1][2] += 1
        else:
            runs.append([position, index, 1])
    return runs


def pieces_of(low, high, local_rows):
    for ahead in range(low // local_rows, (high - 1) // local_rows + 1):
        first = max(low, ahead * local_rows)
        last = min(high, (ahead + 1) * local_rows)
        yield ahead, first - ahead * local_rows, last - first, first - low


def kernel(sizes, needed, by_target, tiles, presence, out, near, ahead_far, behind_far, squared, done,
           send_sem, near_sem, ahead_sem, behind_sem, out_send_sem, out_sem):
    groups, columns, layers, local_rows, rows, part, size = sizes
    me_layer = lax.axis_index("layer")
    me_group = lax.axis_index("row") * columns + lax.axis_index("col")

    def device(steps, layer):
        group = lax.rem(me_group + steps % groups, groups)
        return {"row": lax.div(group, columns), "col": lax.rem(group, columns), "layer": layer}

    everything = list(range(len(by_target)))
    windows = [
        (near, near_sem, -BAND, 2 * BAND, everything),
        (ahead_far, ahead_sem, FAR - 1, 2, needed[0]),
        (behind_far, behind_sem, -FAR - 1, 2, needed[1]),
    ]
    chunks = CHUNKS if rows % CHUNKS == 0 else rows
    step_rows = rows // chunks

    def chunk_rows(chunk, extra):
        first = 0 if chunk == 0 else chunk * step_rows + extra
        return first, (chunk + 1) * step_rows + extra

    def copies_to(chunk, layer, act_remote, act_local):
        for window, sem, low, extra, diagonals in windows:
            first, last = chunk_rows(chunk, extra)
            start_row = low + layer * rows
            for steps, source_row, count, window_row in pieces_of(
                start_row + first, start_row + last, local_rows
            ):
                for position, index, length in runs_of(diagonals):
                    source = tiles.at[pl.ds(index, length), pl.ds(source_row, count)]
                    target = window.at[me_layer, pl.ds(position, length), pl.ds(first + window_row, count)]

                    def remote():
                        act_remote(
                            pltpu.make_async_remote_copy(
                                src_ref=source, dst_ref=target, send_sem=send_sem, recv_sem=sem.at[chunk],
                                device_id=device(-steps, layer), device_id_type=MESH,
                            )
                        )

                    def local():
                        if act_local is not None:
                            act_local(pltpu.make_async_copy(source, target, sem.at[chunk]))

                    if steps % groups == 0:
                        pl.when(me_layer != layer)(remote)
                        pl.when(me_layer == layer)(local)
                    else:
                        remote()

    def start(copy):
        copy.start()

    for chunk in range(chunks):
        for turn in range(layers):
            for layer in range(layers):

                @pl.when(lax.rem(me_layer + turn, layers) == layer)
                def _():
                    copies_to(chunk, layer, start, start)

    def wait_for(chunk):
        for window, sem, _, extra, _ in windows:
            first, last = chunk_rows(chunk, extra)
            arrived = window.at[:, :, pl.ds(first, last - first)]
            pltpu.make_async_copy(arrived, arrived, sem.at[chunk]).wait()

    def tile_of(window, index, row):
        return jnp.concatenate([window[layer, index, row] for layer in range(layers)], axis=0)

    def right_tile(left, right, row):
        if left < WIDTH:
            return tile_of(near, right, row + left)
        if left < WIDTH + 3:
            return tile_of(ahead_far, needed[0].index(right), row + left - WIDTH)
        return tile_of(behind_far, needed[1].index(right), row + left - WIDTH - 3)

    couples = [(0, 1), (2, 3), (4, 5), (6,), (7, 8), (9,), (10, 11), (12,)]

    def product(left_tile, row, finish):
        for couple in couples:
            tables = [dict(by_target[target]) for target in couple]
            lefts = sorted(set(left for table in tables for left in table))
            lhs = jnp.concatenate([left_tile(left) for left in lefts], axis=1)
            rhs = jnp.concatenate(
                [
                    jnp.concatenate(
                        [
                            right_tile(left, table[left], row)
                            if left in table
                            else jnp.zeros((size, size), jnp.bfloat16)
                            for table in tables
                        ],
                        axis=1,
                    )
                    for left in lefts
                ],
                axis=0,
            )
            total = jnp.dot(lhs, rhs, preferred_element_type=jnp.float32)
            for place, target in enumerate(couple):
                finish(target, total[:, place * size : (place + 1) * size])

    def each_result(row, act_remote, act_local):
        place = me_layer * rows + row
        for layer in range(layers):
            source = done.at[row, layer]
            target = out.at[:, place]

            def remote():
                act_remote(
                    pltpu.make_async_remote_copy(
                        src_ref=source, dst_ref=target, send_sem=out_send_sem, recv_sem=out_sem,
                        device_id=device(0, layer), device_id_type=MESH,
                    )
                )

            def local():
                if act_local is not None:
                    act_local(pltpu.make_async_copy(source, target, out_sem))

            pl.when(me_layer != layer)(remote)
            pl.when(me_layer == layer)(local)

    @pl.loop(0, rows)
    def _(row):
        for chunk in range(chunks):

            @pl.when(row == chunk * step_rows)
            def _():
                wait_for(chunk)

        def weight(target):
            return presence[target, me_layer * rows + row].astype(jnp.float32)

        def store_square(target, total):
            squared[target] = (total * weight(target)).astype(jnp.bfloat16)

        def store_result(target, total):
            third = total * weight(target)
            result = (3.0 * squared[target].astype(jnp.float32) - 2.0 * third).astype(jnp.bfloat16)
            for layer in range(layers):
                done[row, layer, target] = result[layer * part : (layer + 1) * part]

        product(lambda left: tile_of(near, left, row + BAND), row, store_square)
        product(lambda left: squared[left], row, store_result)

        @pl.when(row > 0)
        def _():
            each_result(row - 1, start, start)

    each_result(rows - 1, start, start)
    for chunk in range(chunks):
        for layer in range(layers):
            copies_to(chunk, layer, lambda copy: copy.wait_send(), None)

    @pl.loop(0, rows)
    def _(row):
        each_result(row, lambda copy: copy.wait_send(), None)

    pltpu.make_async_copy(out, out, out_sem).wait()


def solution(mesh):
    columns = mesh.shape["col"]
    layers = mesh.shape["layer"]
    groups = mesh.shape["row"] * columns

    def per_device(blocks, presence):
        diagonals, local_rows, part, size = blocks.shape
        total_rows = local_rows * groups
        rows = local_rows // layers
        offsets = offset_table(total_rows)
        by_target = pair_table(offsets, total_rows)
        needed = []
        for first in (WIDTH, WIDTH + 3):
            lefts = range(first, first + 3)
            needed.append(sorted(set(b for pairs in by_target for a, b in pairs if a in lefts)))
        masked = blocks * presence.astype(jnp.bfloat16)[:, :, None, None]
        sizes = (groups, columns, layers, local_rows, rows, part, size)
        return pl.pallas_call(
            functools.partial(kernel, sizes, needed, by_target),
            out_shape=jax.ShapeDtypeStruct(blocks.shape, jnp.bfloat16),
            in_specs=[pl.BlockSpec(memory_space=pl.ANY), pl.BlockSpec(memory_space=pltpu.SMEM)],
            out_specs=pl.BlockSpec(memory_space=pl.ANY),
            scratch_shapes=[
                pltpu.VMEM((layers, diagonals, rows + 2 * BAND, part, size), jnp.bfloat16),
                pltpu.VMEM((layers, len(needed[0]), rows + 2, part, size), jnp.bfloat16),
                pltpu.VMEM((layers, len(needed[1]), rows + 2, part, size), jnp.bfloat16),
                pltpu.VMEM((diagonals, size, size), jnp.bfloat16),
                pltpu.VMEM((rows, layers, diagonals, part, size), jnp.bfloat16),
                pltpu.SemaphoreType.DMA,
                pltpu.SemaphoreType.DMA((rows,)),
                pltpu.SemaphoreType.DMA((rows,)),
                pltpu.SemaphoreType.DMA((rows,)),
                pltpu.SemaphoreType.DMA,
                pltpu.SemaphoreType.DMA,
            ],
            compiler_params=pltpu.CompilerParams(has_side_effects=True, vmem_limit_bytes=48 * 2**20),
        )(masked, presence)

    return jax.shard_map(
        per_device,
        mesh=mesh,
        in_specs=(P(None, ("row", "col"), "layer", None), P(None, ("row", "col"))),
        out_specs=P(None, ("row", "col"), "layer", None),
        check_vma=False,
    )
```

profile of v0, /device:TPU:1, one launch (start us, length us, event | category | flops | bytes accessed | tf_op | source)
XLA Modules:
  0.0 365.5 jit_solution(14251864586016316982)
XLA Ops:
  0.0 0.7 convert_element_type.3
  0.7 0.0 copy-start
  0.7 6.6 %broadcast_multiply_fusion.tiles = bf16[13,64,32,128]{3,2,1,0:T(8,128)(2,1)} fusion(bf16[13,64,32,128]{3,2,1,0:T(8,128)(2,1)} %param.2, bf16[13,64]{1,0:T(8,128)(2,1)S(1)} %convert_element_type.3), kind=kLoop, calls=%fused_computation | loop fusion | flops 3407872 | bytes 13633152 | tf_op jit(solution)/shard_map/mul | solution.py:232
  7.3 0.0 copy-done
  7.3 351.1 %shard_map.28 = bf16[13,64,32,128]{3,2,1,0:T(8,128)(2,1)} custom-call(bf16[13,64,32,128]{3,2,1,0:T(8,128)(2,1)} %broadcast_multiply_fusion.tiles, s32[13,64]{1,0:T(8,128)S(1)} %copy-done), custom_call_target="tpu_custom_call" | custom-call | tf_op jit(solution)/shard_map/pallas_call | solution.py:234
  358.4 7.1 %copy.4 = bf16[13,64,32,128]{3,2,1,0:T(8,128)(2,1)} copy(bf16[13,64,32,128]{3,2,1,0:T(8,128)(2,1)} %shard_map.28) | data formatting | bytes 13631488
Async XLA Ops:
  0.7 6.6 %copy-start = (s32[13,64]{1,0:T(8,128)S(1)}, s32[13,64]{1,0:T(8,128)}, u32[]{:S(2)}) copy-start(s32[13,64]{1,0:T(8,128)} %presence.1) | copy-start | bytes 9988
where the time goes:
time: 371 us; the launch traced here: 366 us
  Pallas kernels  351 us (95%)
  other arithmetic  7.29 us (2%)
  local copies, waits for them, and re-layouts  7.12 us (2%)
    pallas_call x1, Pallas kernels, per_device(): pl.pallas_call(functools.partial(kernel, sizes, needed, by_target), out_s...  351 us

commit v1 on v0

--- a/solution.py
+++ b/solution.py
@@ -1,4 +1,5 @@
 import functools
+import math
 
 import jax
 import jax.numpy as jnp
@@ -10,6 +11,7 @@
 BAND = 3
 FAR = 160
 CHUNKS = 8
+LAG = 2
 WIDTH = 2 * BAND + 1
 MESH = pl.DeviceIdType.MESH
 
@@ -49,7 +51,7 @@
         yield ahead, first - ahead * local_rows, last - first, first - low
 
 
-def kernel(sizes, needed, by_target, tiles, presence, out, near, ahead_far, behind_far, squared, done,
+def direct_kernel(sizes, needed, by_target, tiles, presence, out, near, ahead_far, behind_far, squared, done,
            send_sem, near_sem, ahead_sem, behind_sem, out_send_sem, out_sem):
     groups, columns, layers, local_rows, rows, part, size = sizes
     me_layer = lax.axis_index("layer")
@@ -214,6 +216,379 @@
     pltpu.make_async_copy(out, out, out_sem).wait()
 
 
+def relay_kernel(sizes, needed, by_target, tiles, presence, out, near, ahead, behind, squared, done,
+                 send_sem, near_sem, near_edge_sem, far_band_sem, far_rest_sem, far_edge_sem, out_send_sem, out_sem):
+    groups, columns, layers, local_rows, period, run, part, size = sizes
+    steps = 2 * run
+    distance = FAR // period
+    band_first, band_count, rest_ahead, rest_behind = needed
+    far_count = band_count + 3
+    me_layer = lax.axis_index("layer")
+    me_group = lax.axis_index("row") * columns + lax.axis_index("col")
+    me_column = lax.axis_index("col")
+    windows = (ahead, behind)
+
+    def start(copy):
+        copy.start()
+
+    def wait_send(copy):
+        copy.wait_send()
+
+    def remote(source, target, sem, group, layer, act, sent=send_sem):
+        group = lax.rem(group + 2 * groups, groups)
+        act(
+            pltpu.make_async_remote_copy(
+                src_ref=source, dst_ref=target, send_sem=sent, recv_sem=sem,
+                device_id={"row": lax.div(group, columns), "col": lax.rem(group, columns), "layer": layer},
+                device_id_type=MESH,
+            )
+        )
+
+    def arrived(view, sem):
+        pltpu.make_async_copy(view, view, sem).wait()
+
+    mine = pl.ds(pl.multiple_of(me_layer * part, part), part)
+
+    def near_copies(half, place, first, count, sem, act, act_local):
+        for turn in range(layers):
+            layer = lax.rem(me_layer + turn, layers)
+            row = half * period + layer * run + place - BAND
+            ahead_groups = lax.div(row + local_rows, local_rows) - 1
+            source = tiles.at[pl.ds(first, count), row - ahead_groups * local_rows]
+            target = near.at[half, pl.ds(first, count), place, mine]
+
+            def send():
+                remote(source, target, sem, me_group - ahead_groups, layer, act)
+
+            def local():
+                if act_local is not None:
+                    act_local(pltpu.make_async_copy(source, target, sem))
+
+            if turn == 0:
+                pl.when(ahead_groups != 0)(send)
+                pl.when(ahead_groups == 0)(local)
+            else:
+                send()
+
+    def edge_pieces(side):
+        for position in range(BAND):
+            place = position if side == 0 else run + BAND + position
+            used = set()
+            for pairs in by_target:
+                for left, right in pairs:
+                    if left < WIDTH and 0 <= place - left < run:
+                        used.add(right)
+            for piece, (_, first, count) in enumerate(runs_of(sorted(used))):
+                yield side * BAND + position, place, piece, first, count
+
+    def near_edges(side, act, act_local):
+        for edge, place, piece, first, count in edge_pieces(side):
+            for half in range(2):
+                near_copies(half, place, first, count, near_edge_sem.at[half, edge, piece], act, act_local)
+
+    def wait_near_edges(half, side):
+        for edge, place, piece, first, count in edge_pieces(side):
+            arrived(near.at[half, pl.ds(first, count), place], near_edge_sem.at[half, edge, piece])
+
+    def row_of(step):
+        return lax.rem(step + run - 1, run)
+
+    def near_core(step, act, act_local):
+        row = row_of(step)
+        for half in range(2):
+            near_copies(half, row + BAND, 0, len(by_target), near_sem.at[half, row], act, act_local)
+
+    def each_near(act, act_local):
+        @pl.loop(0, run)
+        def _(step):
+            near_core(step, act, act_local)
+
+            @pl.when(step == 2)
+            def _():
+                near_edges(0, act, act_local)
+
+        near_edges(1, act, act_local)
+
+    def moves(phase):
+        lower = (-distance // 2, (1 - distance) // 2)
+        upper = (distance // 2, (1 + distance) // 2)
+        return (
+            jnp.where(phase == 0, lower[0], lower[1]),
+            jnp.where(phase == 0, upper[0], upper[1]),
+        )
+
+    def relays(phase, column):
+        down, up = moves(phase)
+        column = lax.rem(column + 4 * groups, columns)
+        first = lax.rem(column + down + 4 * groups, columns) - column
+        second = lax.rem(column + up + 4 * groups, columns) - column
+        alike = first * second > 0
+        first, second = jnp.abs(first), jnp.abs(second)
+        return alike & (first <= second), alike & (second < first)
+
+    def far_sends(step, act):
+        phase = lax.div(step, run)
+        row = row_of(step)
+        half = 1 - phase
+        shifts = moves(phase)
+        passes = relays(phase, me_column)
+        band = near.at[phase, pl.ds(band_first, band_count), row + BAND]
+        for side, rest in enumerate((rest_ahead, rest_behind)):
+            group = me_group + shifts[side]
+
+            @pl.when(jnp.logical_not(passes[1 - side]))
+            def _():
+                remote(band, windows[side].at[half, pl.ds(0, band_count), row + 1],
+                       far_band_sem.at[side, half, row], group, me_layer, act)
+
+            remote(near.at[phase, pl.ds(rest, 3), row + BAND],
+                   windows[side].at[half, pl.ds(band_count, 3), row + 1],
+                   far_rest_sem.at[side, half, row], group, me_layer, act)
+
+    def far_relays(step, act, wait):
+        phase = lax.div(step, run)
+        row = row_of(step)
+        half = 1 - phase
+        shifts = moves(phase)
+        passing = [relays(phase, me_column - shifts[side])[side] for side in range(2)]
+        for side in range(2):
+
+            @pl.when(passing[side])
+            def _():
+                view = windows[side].at[half, pl.ds(0, band_count), row + 1]
+                if wait:
+                    arrived(view, far_band_sem.at[side, half, row])
+                remote(view, windows[1 - side].at[half, pl.ds(0, band_count), row + 1],
+                       far_band_sem.at[1 - side, half, row],
+                       me_group - shifts[side] + shifts[1 - side], me_layer, act)
+
+        if wait:
+            for side in range(2):
+
+                @pl.when(jnp.logical_not(passing[side]))
+                def _():
+                    arrived(windows[side].at[half, pl.ds(0, band_count), row + 1], far_band_sem.at[side, half, row])
+
+                arrived(windows[side].at[half, pl.ds(band_count, 3), row + 1], far_rest_sem.at[side, half, row])
+
+    middle = band_count // 2
+    left_edge = [(middle, far_count - middle)]
+    right_edge = [(0, middle + 1), (band_count, 3)]
+
+    def far_edges(step, act):
+        half = 1 - lax.div(step, run)
+        place = lax.rem(step, run)
+        for which, pieces in enumerate((left_edge, right_edge)):
+
+            @pl.when(place == which)
+            def _():
+                if which == 0:
+                    over = me_layer == layers - 1
+                    layer = jnp.where(over, 0, me_layer + 1)
+                    window = half + jnp.where(over, 1, 0)
+                else:
+                    over = me_layer == 0
+                    layer = jnp.where(over, layers - 1, me_layer - 1)
+                    window = half - jnp.where(over, 1, 0)
+                shift = lax.div(window + 2, 2) - 1
+                target_half = window - 2 * shift
+                source_row, target_row = (run, 0) if which == 0 else (1, run + 1)
+                for side in range(2):
+                    for piece, (first, count) in enumerate(pieces):
+                        remote(windows[side].at[half, pl.ds(first, count), source_row],
+                               windows[side].at[target_half, pl.ds(first, count), target_row],
+                               far_edge_sem.at[side, target_half, which + piece],
+                               me_group + shift, layer, act)
+
+    def wait_far_edges(half, which):
+        for side in range(2):
+            for piece, (first, count) in enumerate((left_edge, right_edge)[which]):
+                arrived(windows[side].at[half, pl.ds(first, count), 0 if which == 0 else run + 1],
+                        far_edge_sem.at[side, half, which + piece])
+
+    far_index = [
+        list(range(band_first, band_first + band_count)) + list(range(rest, rest + 3))
+        for rest in (rest_ahead, rest_behind)
+    ]
+
+    def right_tile(left, right, half, row):
+        if left < WIDTH:
+            return near[half, right, row + left]
+        if left < WIDTH + 3:
+            return ahead[half, far_index[0].index(right), row + left - WIDTH]
+        return behind[half, far_index[1].index(right), row + left - WIDTH - 3]
+
+    couples = [(0, 1), (2, 3), (4, 5), (6,), (7, 8), (9,), (10, 11), (12,)]
+
+    def product(left_tile, half, row, finish):
+        for couple in couples:
+            tables = [dict(by_target[target]) for target in couple]
+            lefts = sorted(set(left for table in tables for left in table))
+            lhs = jnp.concatenate([left_tile(left) for left in lefts], axis=1)
+            rhs = jnp.concatenate(
+                [
+                    jnp.concatenate(
+                        [
+                            right_tile(left, table[left], half, row)
+                            if left in table
+                            else jnp.zeros((size, size), jnp.bfloat16)
+                            for table in tables
+                        ],
+                        axis=1,
+                    )
+                    for left in lefts
+                ],
+                axis=0,
+            )
+            total = jnp.dot(lhs, rhs, preferred_element_type=jnp.float32)
+            for place, target in enumerate(couple):
+                finish(target, total[:, place * size : (place + 1) * size])
+
+    def row_at(position):
+        inner = position < run - 2
+        ends = jnp.logical_and(position >= run - 2, position < run)
+        half = jnp.where(position < run, 1, 0)
+        row = jnp.where(inner, position + 1, jnp.where(ends, (position - run + 2) * (run - 1), position - run))
+        return half, row
+
+    def computed_after(step):
+        place = lax.rem(step, run)
+        last = jnp.where(place == run - 1, 1, 0)
+        early = jnp.where(place < 3, 0, place - 2) + last
+        late = jnp.where(place < 2, run - 2, run + place - 1 + 2 * last)
+        return jnp.where(step < 0, 0, jnp.where(step < run, early, late))
+
+    def compute(position):
+        half, row = row_at(position)
+        for at, wait in (
+            (0, lambda: wait_near_edges(1, 0)),
+            (run - 4, lambda: wait_near_edges(1, 1)),
+            (run - 2, lambda: wait_far_edges(1, 0)),
+            (run - 1, lambda: wait_far_edges(1, 1)),
+            (run, lambda: (wait_near_edges(0, 0), wait_far_edges(0, 0))),
+            (2 * run - 3, lambda: wait_near_edges(0, 1)),
+            (2 * run - 1, lambda: wait_far_edges(0, 1)),
+        ):
+
+            @pl.when(position == at)
+            def _():
+                wait()
+
+        global_row = half * period + me_layer * run + row
+
+        def weight(target):
+            return presence[target, global_row].astype(jnp.float32)
+
+        def store_square(target, total):
+            squared[target] = (total * weight(target)).astype(jnp.bfloat16)
+
+        def store_result(target, total):
+            third = total * weight(target)
+            result = (3.0 * squared[target].astype(jnp.float32) - 2.0 * third).astype(jnp.bfloat16)
+            for layer in range(layers):
+                done[position, layer, target] = result[layer * part : (layer + 1) * part]
+
+        product(lambda left: near[half, left, row + BAND], half, row, store_square)
+        product(lambda left: squared[left], half, row, store_result)
+
+    def each_result(position, act, act_local):
+        half, row = row_at(position)
+        target = out.at[:, half * period + me_layer * run + row]
+        for turn in range(layers):
+            layer = lax.rem(me_layer + turn, layers)
+            source = done.at[position, layer]
+            if turn == 0:
+                if act_local is not None:
+                    act_local(pltpu.make_async_copy(source, target, out_sem))
+            else:
+                remote(source, target, out_sem, me_group, layer, act, out_send_sem)
+
+    each_near(start, start)
+
+    @pl.loop(0, steps + LAG)
+    def _(step):
+        @pl.when(step < run)
+        def _():
+            row = row_of(step)
+            for half in range(2):
+                arrived(near.at[half, :, row + BAND], near_sem.at[half, row])
+
+        @pl.when(step < steps)
+        def _():
+            far_sends(step, start)
+
+        @pl.when(step >= LAG)
+        def _():
+            settled = step - LAG
+            far_relays(settled, start, True)
+            far_edges(settled, start)
+
+            @pl.loop(computed_after(settled - 1), computed_after(settled))
+            def _(position):
+                compute(position)
+
+                @pl.when(position > 0)
+                def _():
+                    each_result(position - 1, start, start)
+
+    each_result(steps - 1, start, start)
+    each_near(wait_send, None)
+
+    @pl.loop(0, steps)
+    def _(step):
+        far_sends(step, wait_send)
+        far_relays(step, wait_send, False)
+        far_edges(step, wait_send)
+        each_result(step, wait_send, None)
+
+    arrived(out, out_sem)
+
+
+def relay_plan(groups, local_rows, layers, by_target):
+    total_rows = groups * local_rows
+    period = math.gcd(FAR, total_rows)
+    if local_rows != 2 * period or period % layers or (FAR // period) % 2 == 0 or period // layers < 2 * BAND:
+        return None
+    by_side = []
+    for first in (WIDTH, WIDTH + 3):
+        lefts = range(first, first + 3)
+        by_side.append(set(b for pairs in by_target for a, b in pairs if a in lefts))
+    band = sorted(b for b in by_side[0] if b < WIDTH)
+    wanted = [set(band) | set(range(WIDTH + 3, WIDTH + 6)), set(band) | set(range(WIDTH, WIDTH + 3))]
+    if by_side != wanted or band != list(range(band[0], band[0] + len(band))):
+        return None
+    return period, period // layers, (band[0], len(band), WIDTH + 3, WIDTH)
+
+
+def relay_call(sizes, needed, by_target, masked, presence):
+    run, part, size = sizes[-3:]
+    diagonals = masked.shape[0]
+    layers = sizes[2]
+    far = needed[1] + 3
+    return pl.pallas_call(
+        functools.partial(relay_kernel, sizes, needed, by_target),
+        out_shape=jax.ShapeDtypeStruct(masked.shape, jnp.bfloat16),
+        in_specs=[pl.BlockSpec(memory_space=pl.ANY), pl.BlockSpec(memory_space=pltpu.SMEM)],
+        out_specs=pl.BlockSpec(memory_space=pl.ANY),
+        scratch_shapes=[
+            pltpu.VMEM((2, diagonals, run + 2 * BAND, size, size), jnp.bfloat16),
+            pltpu.VMEM((2, far, run + 2, size, size), jnp.bfloat16),
+            pltpu.VMEM((2, far, run + 2, size, size), jnp.bfloat16),
+            pltpu.VMEM((diagonals, size, size), jnp.bfloat16),
+            pltpu.VMEM((2 * run, layers, diagonals, part, size), jnp.bfloat16),
+            pltpu.SemaphoreType.DMA,
+            pltpu.SemaphoreType.DMA((2, run)),
+            pltpu.SemaphoreType.DMA((2, 2 * BAND, 3)),
+            pltpu.SemaphoreType.DMA((2, 2, run)),
+            pltpu.SemaphoreType.DMA((2, 2, run)),
+            pltpu.SemaphoreType.DMA((2, 2, 3)),
+            pltpu.SemaphoreType.DMA,
+            pltpu.SemaphoreType.DMA,
+        ],
+        compiler_params=pltpu.CompilerParams(has_side_effects=True, vmem_limit_bytes=52 * 2**20),
+    )(masked, presence)
+
+
 def solution(mesh):
     columns = mesh.shape["col"]
     layers = mesh.shape["layer"]
@@ -225,14 +600,19 @@
         rows = local_rows // layers
         offsets = offset_table(total_rows)
         by_target = pair_table(offsets, total_rows)
+        plan = relay_plan(groups, local_rows, layers, by_target)
+        masked = blocks * presence.astype(jnp.bfloat16)[:, :, None, None]
+        if plan is not None:
+            period, run, needed = plan
+            sizes = (groups, columns, layers, local_rows, period, run, part, size)
+            return relay_call(sizes, needed, by_target, masked, presence)
         needed = []
         for first in (WIDTH, WIDTH + 3):
             lefts = range(first, first + 3)
             needed.append(sorted(set(b for pairs in by_target for a, b in pairs if a in lefts)))
-        masked = blocks * presence.astype(jnp.bfloat16)[:, :, None, None]
         sizes = (groups, columns, layers, local_rows, rows, part, size)
         return pl.pallas_call(
-            functools.partial(kernel, sizes, needed, by_target),
+            functools.partial(direct_kernel, sizes, needed, by_target),
             out_shape=jax.ShapeDtypeStruct(blocks.shape, jnp.bfloat16),
             in_specs=[pl.BlockSpec(memory_space=pl.ANY), pl.BlockSpec(memory_space=pltpu.SMEM)],
             out_specs=pl.BlockSpec(memory_space=pl.ANY),

time: 371 us -> 327 us (0.88); the launches traced: 366 us -> 327 us
  Pallas kernels: 351 us -> 313 us
    pallas_call x1, Pallas kernels: 351 us -> 313 us  [relay_call(): pl.pallas_call(functools.partial(relay_kernel, sizes, needed, by_target),...]
where the time goes in v1:
time: 327 us
  Pallas kernels  313 us (96%)
  other arithmetic  7.29 us (2%)
  local copies, waits for them, and re-layouts  7.12 us (2%)
    pallas_call x1, Pallas kernels, relay_call(): pl.pallas_call(functools.partial(relay_kernel, sizes, needed, by_target),...  313 us
    unnamed x3, local copies, waits for them, and re-layouts  7.12 us
    mul x1, other arithmetic, per_device(): masked = blocks * presence.astype(jnp.bfloat16)[:, :, None, None]  6.59 us

profile of v1, /device:TPU:1, one launch (start us, length us, event | category | flops | bytes accessed | tf_op | source)
XLA Modules:
  0.0 327.0 jit_solution(14561724378499450293)
XLA Ops:
  0.0 0.7 convert_element_type.3
  0.7 0.0 copy-start
  0.7 6.6 %broadcast_multiply_fusion.tiles = bf16[13,64,32,128]{3,2,1,0:T(8,128)(2,1)} fusion(bf16[13,64,32,128]{3,2,1,0:T(8,128)(2,1)} %param.2, bf16[13,64]{1,0:T(8,128)(2,1)S(1)} %convert_element_type.3), kind=kLoop, calls=%fused_computation | loop fusion | flops 3407872 | bytes 13633152 | tf_op jit(solution)/shard_map/mul | solution.py:604
  7.3 0.0 copy-done
  7.3 312.6 %shard_map.28 = bf16[13,64,32,128]{3,2,1,0:T(8,128)(2,1)} custom-call(bf16[13,64,32,128]{3,2,1,0:T(8,128)(2,1)} %broadcast_multiply_fusion.tiles, s32[13,64]{1,0:T(8,128)S(1)} %copy-done), custom_call_target="tpu_custom_call" | custom-call | tf_op jit(solution)/shard_map/pallas_call | solution.py:568
  319.9 7.1 %copy.4 = bf16[13,64,32,128]{3,2,1,0:T(8,128)(2,1)} copy(bf16[13,64,32,128]{3,2,1,0:T(8,128)(2,1)} %shard_map.28) | data formatting | bytes 13631488
Async XLA Ops:
  0.7 6.6 %copy-start = (s32[13,64]{1,0:T(8,128)S(1)}, s32[13,64]{1,0:T(8,128)}, u32[]{:S(2)}) copy-start(s32[13,64]{1,0:T(8,128)} %presence.1) | copy-start | bytes 9988

commit v2 on v1

--- a/solution.py
+++ b/solution.py
@@ -11,7 +11,9 @@
 BAND = 3
 FAR = 160
 CHUNKS = 8
-LAG = 2
+RELAY_LAG = 2
+LAG = 3
+PACE = 1
 WIDTH = 2 * BAND + 1
 MESH = pl.DeviceIdType.MESH
 
@@ -216,8 +218,8 @@
     pltpu.make_async_copy(out, out, out_sem).wait()
 
 
-def relay_kernel(sizes, needed, by_target, tiles, presence, out, near, ahead, behind, squared, done,
-                 send_sem, near_sem, near_edge_sem, far_band_sem, far_rest_sem, far_edge_sem, out_send_sem, out_sem):
+def relay_kernel(sizes, needed, by_target, blocks, presence, out, tiles, near, ahead, behind, squared, done,
+                 load_sem, send_sem, near_sem, near_edge_sem, far_band_sem, far_rest_sem, far_edge_sem, out_send_sem, out_sem):
     groups, columns, layers, local_rows, period, run, part, size = sizes
     steps = 2 * run
     distance = FAR // period
@@ -293,21 +295,55 @@
     def row_of(step):
         return lax.rem(step + run - 1, run)
 
-    def near_core(step, act, act_local):
+    def near_step(step, act, act_local):
+        half = lax.div(step, run)
         row = row_of(step)
-        for half in range(2):
-            near_copies(half, row + BAND, 0, len(by_target), near_sem.at[half, row], act, act_local)
-
-    def each_near(act, act_local):
-        @pl.loop(0, run)
+        near_copies(half, row + BAND, 0, len(by_target), near_sem.at[half, row], act, act_local)
+
+    def own_row(step, layer):
+        return lax.div(step, run) * period + layer * run + row_of(step)
+
+    def loads(step, act):
+        for layer in range(layers):
+            row = own_row(step, layer)
+            act(pltpu.make_async_copy(blocks.at[:, row], tiles.at[:, row], load_sem.at[step, layer]))
+
+    def mask(step):
+        for layer in range(layers):
+            row = own_row(step, layer)
+            for target in range(len(by_target)):
+                weight = presence[target, row].astype(jnp.float32)
+                tiles[target, row] = (tiles[target, row].astype(jnp.float32) * weight).astype(jnp.bfloat16)
+
+    def send_near():
+        @pl.loop(0, steps)
         def _(step):
-            near_core(step, act, act_local)
-
-            @pl.when(step == 2)
-            def _():
-                near_edges(0, act, act_local)
-
-        near_edges(1, act, act_local)
+            loads(step, start)
+
+        @pl.loop(0, steps + 1)
+        def _(step):
+            @pl.when(step < steps)
+            def _():
+                loads(step, lambda copy: copy.wait())
+                mask(step)
+
+            @pl.when(step > 0)
+            def _():
+                near_step(step - 1, start, start)
+
+        for side in range(2):
+            near_edges(side, start, start)
+
+    def wait_near_sends():
+        @pl.loop(0, steps)
+        def _(step):
+            near_step(step, wait_send, None)
+
+        for side in range(2):
+            near_edges(side, wait_send, None)
+
+    def wait_near(half, row):
+        arrived(near.at[half, :, row + BAND], near_sem.at[half, row])
 
     def moves(phase):
         lower = (-distance // 2, (1 - distance) // 2)
@@ -323,8 +359,16 @@
         first = lax.rem(column + down + 4 * groups, columns) - column
         second = lax.rem(column + up + 4 * groups, columns) - column
         alike = first * second > 0
-        first, second = jnp.abs(first), jnp.abs(second)
-        return alike & (first <= second), alike & (second < first)
+        middle = columns // 2
+
+        def crosses(shift):
+            return (column < middle) != (column + shift < middle)
+
+        nearer = jnp.abs(first) <= jnp.abs(second)
+        return (
+            alike & nearer & crosses(first),
+            alike & jnp.logical_not(nearer) & crosses(second),
+        )
 
     def far_sends(step, act):
         phase = lax.div(step, run)
@@ -345,15 +389,18 @@
                    windows[side].at[half, pl.ds(band_count, 3), row + 1],
                    far_rest_sem.at[side, half, row], group, me_layer, act)
 
+    def passes_on(phase):
+        shifts = moves(phase)
+        return [relays(phase, me_column - shifts[side])[side] for side in range(2)]
+
     def far_relays(step, act, wait):
         phase = lax.div(step, run)
         row = row_of(step)
         half = 1 - phase
         shifts = moves(phase)
-        passing = [relays(phase, me_column - shifts[side])[side] for side in range(2)]
-        for side in range(2):
-
-            @pl.when(passing[side])
+        for side, passing in enumerate(passes_on(phase)):
+
+            @pl.when(passing)
             def _():
                 view = windows[side].at[half, pl.ds(0, band_count), row + 1]
                 if wait:
@@ -362,14 +409,17 @@
                        far_band_sem.at[1 - side, half, row],
                        me_group - shifts[side] + shifts[1 - side], me_layer, act)
 
-        if wait:
-            for side in range(2):
-
-                @pl.when(jnp.logical_not(passing[side]))
-                def _():
-                    arrived(windows[side].at[half, pl.ds(0, band_count), row + 1], far_band_sem.at[side, half, row])
-
-                arrived(windows[side].at[half, pl.ds(band_count, 3), row + 1], far_rest_sem.at[side, half, row])
+    def wait_far(step):
+        phase = lax.div(step, run)
+        row = row_of(step)
+        half = 1 - phase
+        for side, passing in enumerate(passes_on(phase)):
+
+            @pl.when(jnp.logical_not(passing))
+            def _():
+                arrived(windows[side].at[half, pl.ds(0, band_count), row + 1], far_band_sem.at[side, half, row])
+
+            arrived(windows[side].at[half, pl.ds(band_count, 3), row + 1], far_rest_sem.at[side, half, row])
 
     middle = band_count // 2
     left_edge = [(middle, far_count - middle)]
@@ -446,31 +496,31 @@
 
     def row_at(position):
         inner = position < run - 2
-        ends = jnp.logical_and(position >= run - 2, position < run)
         half = jnp.where(position < run, 1, 0)
-        row = jnp.where(inner, position + 1, jnp.where(ends, (position - run + 2) * (run - 1), position - run))
-        return half, row
+        ends = jnp.where(position < run, (position - run + 2) * (run - 1), position - run)
+        return half, jnp.where(inner, position + 1, ends)
 
     def computed_after(step):
-        place = lax.rem(step, run)
-        last = jnp.where(place == run - 1, 1, 0)
-        early = jnp.where(place < 3, 0, place - 2) + last
-        late = jnp.where(place < 2, run - 2, run + place - 1 + 2 * last)
-        return jnp.where(step < 0, 0, jnp.where(step < run, early, late))
+        since = step - run
+        early = jnp.where(since < 3, jnp.maximum(since, 0), jnp.minimum(2 * since - 2, run - 2))
+        place = step - LAG - run
+        late = jnp.where(place < 2, run - 1, run + place - 1)
+        late = jnp.where(place >= run - 1, steps, late)
+        return jnp.where(place < 1, early, late)
 
     def compute(position):
         half, row = row_at(position)
-        for at, wait in (
-            (0, lambda: wait_near_edges(1, 0)),
-            (run - 4, lambda: wait_near_edges(1, 1)),
-            (run - 2, lambda: wait_far_edges(1, 0)),
-            (run - 1, lambda: wait_far_edges(1, 1)),
-            (run, lambda: (wait_near_edges(0, 0), wait_far_edges(0, 0))),
-            (2 * run - 3, lambda: wait_near_edges(0, 1)),
-            (2 * run - 1, lambda: wait_far_edges(0, 1)),
+        for at_half, at_row, wait in (
+            (1, 1, lambda: wait_near_edges(1, 0)),
+            (1, run - BAND, lambda: wait_near_edges(1, 1)),
+            (1, 0, lambda: wait_far_edges(1, 0)),
+            (1, run - 1, lambda: wait_far_edges(1, 1)),
+            (0, 0, lambda: (wait_near_edges(0, 0), wait_far_edges(0, 0))),
+            (0, run - BAND, lambda: wait_near_edges(0, 1)),
+            (0, run - 1, lambda: wait_far_edges(0, 1)),
         ):
 
-            @pl.when(position == at)
+            @pl.when(jnp.logical_and(half == at_half, row == at_row))
             def _():
                 wait()
 
@@ -503,27 +553,35 @@
             else:
                 remote(source, target, out_sem, me_group, layer, act, out_send_sem)
 
-    each_near(start, start)
+    send_near()
 
     @pl.loop(0, steps + LAG)
     def _(step):
-        @pl.when(step < run)
+        other = step - run // 2
+
+        @pl.when(jnp.logical_and(other >= 0, other < run))
         def _():
-            row = row_of(step)
-            for half in range(2):
-                arrived(near.at[half, :, row + BAND], near_sem.at[half, row])
-
-        @pl.when(step < steps)
+            wait_near(1, row_of(other))
+
+        @pl.loop(jnp.minimum(PACE * step, steps), jnp.minimum(PACE * (step + 1), steps))
+        def _(sent):
+            @pl.when(sent < run)
+            def _():
+                wait_near(0, row_of(sent))
+
+            far_sends(sent, start)
+
+        @pl.when(jnp.logical_and(step >= RELAY_LAG, step < steps + RELAY_LAG))
         def _():
-            far_sends(step, start)
+            far_relays(step - RELAY_LAG, start, True)
 
         @pl.when(step >= LAG)
         def _():
             settled = step - LAG
-            far_relays(settled, start, True)
+            wait_far(settled)
             far_edges(settled, start)
 
-            @pl.loop(computed_after(settled - 1), computed_after(settled))
+            @pl.loop(computed_after(step - 1), computed_after(step))
             def _(position):
                 compute(position)
 
@@ -532,7 +590,7 @@
                     each_result(position - 1, start, start)
 
     each_result(steps - 1, start, start)
-    each_near(wait_send, None)
+    wait_near_sends()
 
     @pl.loop(0, steps)
     def _(step):
@@ -547,7 +605,7 @@
 def relay_plan(groups, local_rows, layers, by_target):
     total_rows = groups * local_rows
     period = math.gcd(FAR, total_rows)
-    if local_rows != 2 * period or period % layers or (FAR // period) % 2 == 0 or period // layers < 2 * BAND:
+    if local_rows != 2 * period or period % layers or (FAR // period) % 2 == 0 or period // layers < 2 * BAND + 2:
         return None
     by_side = []
     for first in (WIDTH, WIDTH + 3):
@@ -560,22 +618,24 @@
     return period, period // layers, (band[0], len(band), WIDTH + 3, WIDTH)
 
 
-def relay_call(sizes, needed, by_target, masked, presence):
+def relay_call(sizes, needed, by_target, blocks, presence):
     run, part, size = sizes[-3:]
-    diagonals = masked.shape[0]
+    diagonals = blocks.shape[0]
     layers = sizes[2]
     far = needed[1] + 3
     return pl.pallas_call(
         functools.partial(relay_kernel, sizes, needed, by_target),
-        out_shape=jax.ShapeDtypeStruct(masked.shape, jnp.bfloat16),
+        out_shape=jax.ShapeDtypeStruct(blocks.shape, jnp.bfloat16),
         in_specs=[pl.BlockSpec(memory_space=pl.ANY), pl.BlockSpec(memory_space=pltpu.SMEM)],
         out_specs=pl.BlockSpec(memory_space=pl.ANY),
         scratch_shapes=[
+            pltpu.VMEM(blocks.shape, jnp.bfloat16),
             pltpu.VMEM((2, diagonals, run + 2 * BAND, size, size), jnp.bfloat16),
             pltpu.VMEM((2, far, run + 2, size, size), jnp.bfloat16),
             pltpu.VMEM((2, far, run + 2, size, size), jnp.bfloat16),
             pltpu.VMEM((diagonals, size, size), jnp.bfloat16),
             pltpu.VMEM((2 * run, layers, diagonals, part, size), jnp.bfloat16),
+            pltpu.SemaphoreType.DMA((2 * run, layers)),
             pltpu.SemaphoreType.DMA,
             pltpu.SemaphoreType.DMA((2, run)),
             pltpu.SemaphoreType.DMA((2, 2 * BAND, 3)),
@@ -586,7 +646,7 @@
             pltpu.SemaphoreType.DMA,
         ],
         compiler_params=pltpu.CompilerParams(has_side_effects=True, vmem_limit_bytes=52 * 2**20),
-    )(masked, presence)
+    )(blocks, presence)
 
 
 def solution(mesh):
@@ -601,15 +661,15 @@
         offsets = offset_table(total_rows)
         by_target = pair_table(offsets, total_rows)
         plan = relay_plan(groups, local_rows, layers, by_target)
-        masked = blocks * presence.astype(jnp.bfloat16)[:, :, None, None]
         if plan is not None:
             period, run, needed = plan
             sizes = (groups, columns, layers, local_rows, period, run, part, size)
-            return relay_call(sizes, needed, by_target, masked, presence)
+            return relay_call(sizes, needed, by_target, blocks, presence)
         needed = []
         for first in (WIDTH, WIDTH + 3):
             lefts = range(first, first + 3)
             needed.append(sorted(set(b for pairs in by_target for a, b in pairs if a in lefts)))
+        masked = blocks * presence.astype(jnp.bfloat16)[:, :, None, None]
         sizes = (groups, columns, layers, local_rows, rows, part, size)
         return pl.pallas_call(
             functools.partial(direct_kernel, sizes, needed, by_target),

time: 327 us -> 284 us (0.87)
  Pallas kernels: 313 us -> 276 us
  other arithmetic: 7.29 us -> 0 us
    pallas_call x1, Pallas kernels: 313 us -> 276 us  [relay_call(): pl.pallas_call(functools.partial(relay_kernel, sizes, needed, by_target),...]
    mul x1 -> x0, other arithmetic: 6.59 us -> none  [per_device(): masked = blocks * presence.astype(jnp.bfloat16)[:, :, None, None]]
where the time goes in v2:
time: 284 us
  Pallas kernels  276 us (97%)
  local copies, waits for them, and re-layouts  7.81 us (3%)
    pallas_call x1, Pallas kernels, relay_call(): pl.pallas_call(functools.partial(relay_kernel, sizes, needed, by_target),...  276 us
    unnamed x3, local copies, waits for them, and re-layouts  7.81 us

profile of v2, /device:TPU:1, one launch (start us, length us, event | category | flops | bytes accessed | tf_op | source)
XLA Modules:
  0.0 283.8 jit_solution(13928799281247313593)
XLA Ops:
  0.0 0.0 copy-start
  0.0 0.7 copy-done
  0.7 276.0 %shard_map.28 = bf16[13,64,32,128]{3,2,1,0:T(8,128)(2,1)} custom-call(bf16[13,64,32,128]{3,2,1,0:T(8,128)(2,1)} %blocks.1, s32[13,64]{1,0:T(8,128)S(1)} %copy-done), custom_call_target="tpu_custom_call" | custom-call | tf_op jit(solution)/shard_map/pallas_call | solution.py:626
  276.7 7.1 %copy.4 = bf16[13,64,32,128]{3,2,1,0:T(8,128)(2,1)} copy(bf16[13,64,32,128]{3,2,1,0:T(8,128)(2,1)} %shard_map.28) | data formatting | bytes 13631488
Async XLA Ops:
  0.0 0.7 copy-start

commit v3 on v2

--- a/solution.py
+++ b/solution.py
@@ -12,8 +12,10 @@
 FAR = 160
 CHUNKS = 8
 RELAY_LAG = 2
-LAG = 3
-PACE = 1
+LAG = 2
+DIRECT = 1
+FIRST = 16
+RATE = 1
 WIDTH = 2 * BAND + 1
 MESH = pl.DeviceIdType.MESH
 
@@ -315,24 +317,17 @@
                 weight = presence[target, row].astype(jnp.float32)
                 tiles[target, row] = (tiles[target, row].astype(jnp.float32) * weight).astype(jnp.bfloat16)
 
-    def send_near():
-        @pl.loop(0, steps)
+    def prepare(step):
+        @pl.when(step < steps)
+        def _():
+            loads(step, lambda copy: copy.wait())
+            mask(step)
+
+    def send_near(first, last):
+        @pl.loop(first, last)
         def _(step):
-            loads(step, start)
-
-        @pl.loop(0, steps + 1)
-        def _(step):
-            @pl.when(step < steps)
-            def _():
-                loads(step, lambda copy: copy.wait())
-                mask(step)
-
-            @pl.when(step > 0)
-            def _():
-                near_step(step - 1, start, start)
-
-        for side in range(2):
-            near_edges(side, start, start)
+            prepare(step + 2)
+            near_step(step, start, start)
 
     def wait_near_sends():
         @pl.loop(0, steps)
@@ -376,18 +371,31 @@
         half = 1 - phase
         shifts = moves(phase)
         passes = relays(phase, me_column)
-        band = near.at[phase, pl.ds(band_first, band_count), row + BAND]
+
+        def send(side, first, count, place, sem):
+            group = me_group + shifts[side]
+
+            @pl.when(step < DIRECT)
+            def _():
+                for turn in range(layers):
+                    layer = lax.rem(me_layer + turn, layers)
+                    remote(tiles.at[pl.ds(first, count), own_row(step, layer)],
+                           windows[side].at[half, pl.ds(place, count), row + 1, mine],
+                           sem, group, layer, act)
+
+            @pl.when(step >= DIRECT)
+            def _():
+                remote(near.at[phase, pl.ds(first, count), row + BAND],
+                       windows[side].at[half, pl.ds(place, count), row + 1],
+                       sem, group, me_layer, act)
+
         for side, rest in enumerate((rest_ahead, rest_behind)):
-            group = me_group + shifts[side]
 
             @pl.when(jnp.logical_not(passes[1 - side]))
             def _():
-                remote(band, windows[side].at[half, pl.ds(0, band_count), row + 1],
-                       far_band_sem.at[side, half, row], group, me_layer, act)
-
-            remote(near.at[phase, pl.ds(rest, 3), row + BAND],
-                   windows[side].at[half, pl.ds(band_count, 3), row + 1],
-                   far_rest_sem.at[side, half, row], group, me_layer, act)
+                send(side, band_first, band_count, 0, far_band_sem.at[side, half, row])
+
+            send(side, rest, 3, band_count, far_rest_sem.at[side, half, row])
 
     def passes_on(phase):
         shifts = moves(phase)
@@ -553,7 +561,15 @@
             else:
                 remote(source, target, out_sem, me_group, layer, act, out_send_sem)
 
-    send_near()
+    @pl.loop(0, steps)
+    def _(step):
+        loads(step, start)
+
+    for step in range(2):
+        prepare(step)
+
+    def near_until(step):
+        return jnp.where(step < 0, 0, jnp.minimum(FIRST + RATE * step, steps))
 
     @pl.loop(0, steps + LAG)
     def _(step):
@@ -563,13 +579,29 @@
         def _():
             wait_near(1, row_of(other))
 
-        @pl.loop(jnp.minimum(PACE * step, steps), jnp.minimum(PACE * (step + 1), steps))
-        def _(sent):
-            @pl.when(sent < run)
-            def _():
-                wait_near(0, row_of(sent))
-
-            far_sends(sent, start)
+        @pl.when(step < DIRECT)
+        def _():
+            far_sends(step, start)
+
+        send_near(near_until(step - 1), near_until(step))
+
+        @pl.when(jnp.logical_and(near_until(step - 1) < steps, near_until(step) == steps))
+        def _():
+            for side in range(2):
+                near_edges(side, start, start)
+
+        @pl.when(jnp.logical_and(step >= DIRECT, step < steps))
+        def _():
+            @pl.when(step < run)
+            def _():
+                wait_near(0, row_of(step))
+
+            far_sends(step, start)
+
+        @pl.when(step == run)
+        def _():
+            for early in range(DIRECT):
+                wait_near(0, row_of(jnp.int32(early)))
 
         @pl.when(jnp.logical_and(step >= RELAY_LAG, step < steps + RELAY_LAG))
         def _():
@@ -625,9 +657,9 @@
     far = needed[1] + 3
     return pl.pallas_call(
         functools.partial(relay_kernel, sizes, needed, by_target),
-        out_shape=jax.ShapeDtypeStruct(blocks.shape, jnp.bfloat16),
+        out_shape=pltpu.VMEM(blocks.shape, jnp.bfloat16),
         in_specs=[pl.BlockSpec(memory_space=pl.ANY), pl.BlockSpec(memory_space=pltpu.SMEM)],
-        out_specs=pl.BlockSpec(memory_space=pl.ANY),
+        out_specs=pl.BlockSpec(memory_space=pltpu.VMEM),
         scratch_shapes=[
             pltpu.VMEM(blocks.shape, jnp.bfloat16),
             pltpu.VMEM((2, diagonals, run + 2 * BAND, size, size), jnp.bfloat16),
@@ -645,7 +677,7 @@
             pltpu.SemaphoreType.DMA,
             pltpu.SemaphoreType.DMA,
         ],
-        compiler_params=pltpu.CompilerParams(has_side_effects=True, vmem_limit_bytes=52 * 2**20),
+        compiler_params=pltpu.CompilerParams(has_side_effects=True, vmem_limit_bytes=44 * 2**20),
     )(blocks, presence)
 
 

time: 284 us -> 275 us (0.968)
  Pallas kernels: 276 us -> 270 us
  local copies, waits for them, and re-layouts: 7.81 us -> 3.57 us
    pallas_call x1, Pallas kernels: 276 us -> 270 us  [relay_call(): pl.pallas_call(functools.partial(relay_kernel, sizes, needed, by_target),...]
    unnamed x3, local copies, waits for them, and re-layouts: 7.81 us -> 3.57 us
where the time goes in v3:
time: 275 us; the launch traced here: 274 us
  Pallas kernels  270 us (98%)
  local copies, waits for them, and re-layouts  3.57 us (1%)
    pallas_call x1, Pallas kernels, relay_call(): pl.pallas_call(functools.partial(relay_kernel, sizes, needed, by_target),...  270 us

profile of v3, /device:TPU:1, one launch (start us, length us, event | category | flops | bytes accessed | tf_op | source)
XLA Modules:
  0.0 273.9 jit_solution(15460879466594195396)
XLA Ops:
  0.0 0.0 copy-start
  0.0 0.7 copy-done
  0.7 270.3 %shard_map.28 = bf16[13,64,32,128]{3,2,1,0:T(8,128)(2,1)S(1)} custom-call(bf16[13,64,32,128]{3,2,1,0:T(8,128)(2,1)} %blocks.1, s32[13,64]{1,0:T(8,128)S(1)} %copy-done), custom_call_target="tpu_custom_call" | custom-call | tf_op jit(solution)/shard_map/pallas_call | solution.py:658
  271.0 2.9 %copy.4 = bf16[13,64,32,128]{3,2,1,0:T(8,128)(2,1)} copy(bf16[13,64,32,128]{3,2,1,0:T(8,128)(2,1)S(1)} %shard_map.28) | data formatting | bytes 13631488
Async XLA Ops:
  0.0 0.7 copy-start

commit v4 on v3

--- a/solution.py
+++ b/solution.py
@@ -12,7 +12,7 @@
 FAR = 160
 CHUNKS = 8
 RELAY_LAG = 2
-LAG = 2
+LAG = 3
 DIRECT = 1
 FIRST = 16
 RATE = 1
@@ -389,13 +389,18 @@
                        windows[side].at[half, pl.ds(place, count), row + 1],
                        sem, group, me_layer, act)
 
-        for side, rest in enumerate((rest_ahead, rest_behind)):
-
+        def send_side(side):
             @pl.when(jnp.logical_not(passes[1 - side]))
             def _():
                 send(side, band_first, band_count, 0, far_band_sem.at[side, half, row])
 
-            send(side, rest, 3, band_count, far_rest_sem.at[side, half, row])
+            send(side, (rest_ahead, rest_behind)[side], 3, band_count, far_rest_sem.at[side, half, row])
+
+        cores = [lax.div(lax.rem(me_group + shift + 2 * groups, groups), columns) for shift in shifts]
+        later = cores[0] < cores[1]
+        pl.when(jnp.logical_not(later))(lambda: send_side(0))
+        send_side(1)
+        pl.when(later)(lambda: send_side(0))
 
     def passes_on(phase):
         shifts = moves(phase)

time: 275 us -> 273 us (level)
  no operation moved by 1% of the time
where the time goes in v4:
time: 273 us; the launch traced here: 272 us
  Pallas kernels  269 us (99%)
  local copies, waits for them, and re-layouts  3.57 us (1%)
    pallas_call x1, Pallas kernels, relay_call(): pl.pallas_call(functools.partial(relay_kernel, sizes, needed, by_target),...  269 us

profile of v4, /device:TPU:1, one launch (start us, length us, event | category | flops | bytes accessed | tf_op | source)
XLA Modules:
  0.0 272.3 jit_solution(12175806514111232747)
XLA Ops:
  0.0 0.0 copy-start
  0.0 0.7 copy-done
  0.7 268.8 %shard_map.28 = bf16[13,64,32,128]{3,2,1,0:T(8,128)(2,1)S(1)} custom-call(bf16[13,64,32,128]{3,2,1,0:T(8,128)(2,1)} %blocks.1, s32[13,64]{1,0:T(8,128)S(1)} %copy-done), custom_call_target="tpu_custom_call" | custom-call | tf_op jit(solution)/shard_map/pallas_call | solution.py:663
  269.5 2.9 %copy.4 = bf16[13,64,32,128]{3,2,1,0:T(8,128)(2,1)} copy(bf16[13,64,32,128]{3,2,1,0:T(8,128)(2,1)S(1)} %shard_map.28) | data formatting | bytes 13631488
Async XLA Ops:
  0.0 0.7 copy-start

commit v5 on v4

--- a/solution.py
+++ b/solution.py
@@ -590,7 +590,7 @@
 
         send_near(near_until(step - 1), near_until(step))
 
-        @pl.when(jnp.logical_and(near_until(step - 1) < steps, near_until(step) == steps))
+        @pl.when(step == 1)
         def _():
             for side in range(2):
                 near_edges(side, start, start)

time: 273 us -> 272 us (level)
  no operation moved by 1% of the time
where the time goes in v5:
time: 272 us
  Pallas kernels  269 us (99%)
  local copies, waits for them, and re-layouts  3.57 us (1%)
    pallas_call x1, Pallas kernels, relay_call(): pl.pallas_call(functools.partial(relay_kernel, sizes, needed, by_target),...  269 us

profile of v5, /device:TPU:1, one launch (start us, length us, event | category | flops | bytes accessed | tf_op | source)
XLA Modules:
  0.0 272.3 jit_solution(15331646178661105339)
XLA Ops:
  0.0 0.0 copy-start
  0.0 0.7 copy-done
  0.7 268.7 %shard_map.28 = bf16[13,64,32,128]{3,2,1,0:T(8,128)(2,1)S(1)} custom-call(bf16[13,64,32,128]{3,2,1,0:T(8,128)(2,1)} %blocks.1, s32[13,64]{1,0:T(8,128)S(1)} %copy-done), custom_call_target="tpu_custom_call" | custom-call | tf_op jit(solution)/shard_map/pallas_call | solution.py:663
  269.4 2.9 %copy.4 = bf16[13,64,32,128]{3,2,1,0:T(8,128)(2,1)} copy(bf16[13,64,32,128]{3,2,1,0:T(8,128)(2,1)S(1)} %shard_map.28) | data formatting | bytes 13631488
Async XLA Ops:
  0.0 0.7 copy-start
